TPU v7x, 128 devices: a whole 4x4x4 slice. The times are simulated.
128 devices in a mesh: blk: 16 (over x_hi, z, core), uly: 8 (over x_lo, y).
Axes of the slice: x: 4 (x_hi: 2, x_lo: 2; x = x_hi * 2 + x_lo), y: 4, z: 4, core: 2. Of those that a mesh axis runs over, the one named last changes fastest.
Arguments:
- queries: bfloat16 [32768, 4096], P(('blk', 'uly')), may hold values from -140 to 140
- keys: bfloat16 [32768, 1024], P(('blk', 'uly')), may hold values from -6 to 6
- values: bfloat16 [32768, 1024], P(('blk', 'uly')), may hold values from -6 to 6
- doc_lengths: int32 [4], replicated, may hold values from 1 to 24576, 32768 in all
- selected: int32 [32, 8], replicated, may hold values from 0 to 30, as said below
Outputs:
- attended: bfloat16 [32768, 4096], P(('blk', 'uly'))
Inputs may be any that keep to these rules, and one draw needn't show every extreme that they name: selected[b, g] <= b, and equals b only for b = 0. For every device index along blk (blocks b with equal b // 2) and every key head, the blocks it selects that lie outside its own 2 blocks lie in distinct blocks of blk, so one other index of blk supplies at most one selected block a key head to it.
All inputs are finite; a program needn't handle non-finite values.
Results may differ from a plain program's by a relative error of at most 0.004.
Values may be sent and summed in bfloat16 or wider, within the bound.
A program may use at most 128 MiB of HBM per device.

v0:
```python
import jax
import jax.numpy as jnp
from jax import lax
from jax.sharding import PartitionSpec as P

HQ = 32
KVH = 8
HD = 128
MB = 1024


def shortened(shard):

    def short(part):
        return part.astype(jnp.bfloat16) if part.dtype == jnp.float32 else part

    return jax.tree.map(short, shard)


def on_device(queries, keys, values, doc_lengths, selected):
    q_heads, k_heads, v_heads = (
        lax.all_to_all(queries, "uly", split_axis=1, concat_axis=0, tiled=True),
        lax.all_to_all(keys, "uly", split_axis=1, concat_axis=0, tiled=True),
        lax.all_to_all(values, "uly", split_axis=1, concat_axis=0, tiled=True),
    )
    shard = k_heads.shape[0]
    kv_dev = k_heads.shape[1] // HD
    per_dev = shard // MB
    group = HQ // KVH
    scale = 1.0 / HD**0.5
    blk_index = lax.axis_index("blk")
    uly_index = lax.axis_index("uly")
    ends = jnp.cumsum(doc_lengths)

    def doc_of(places):
        return jnp.sum((ends <= places[..., None]).astype(jnp.int32), axis=-1)

    column = lax.dynamic_slice_in_dim(selected, uly_index * kv_dev, kv_dev, 1)
    mine = lax.dynamic_slice_in_dim(column, blk_index * per_dev, per_dev, 0)
    offsets = jnp.arange(MB, dtype=jnp.int32)
    k_blocks = k_heads.reshape(per_dev, MB, kv_dev, HD)
    v_blocks = v_heads.reshape(per_dev, MB, kv_dev, HD)
    empty = jnp.zeros((per_dev, kv_dev, MB, HD), jnp.bfloat16)
    k_piece = lax.all_gather(k_heads, "blk", axis=0, tiled=True)
    v_piece = lax.all_gather(v_heads, "blk", axis=0, tiled=True)
    count = k_piece.shape[0]
    wanted_rows = mine[:, :, None] * MB + offsets
    inside = (wanted_rows >= 0) & (wanted_rows < count)
    index = jnp.clip(wanted_rows, 0, count - 1)
    head_rows = jnp.arange(kv_dev, dtype=jnp.int32)[None, :, None]
    k_got = k_piece.reshape(count, kv_dev, HD)[index, head_rows]
    v_got = v_piece.reshape(count, kv_dev, HD)[index, head_rows]
    chosen_k = jnp.where(inside[..., None], k_got, empty)
    chosen_v = jnp.where(inside[..., None], v_got, empty)
    doc_query = doc_of(blk_index * shard + jnp.arange(shard, dtype=jnp.int32)).reshape(per_dev, MB)
    doc_chosen = doc_of(mine[:, :, None] * MB + offsets)
    live = mine != (blk_index * per_dev + jnp.arange(per_dev, dtype=jnp.int32))[:, None]
    q_five = q_heads.reshape(per_dev, MB, kv_dev, group, HD)
    causal = offsets[:, None] >= offsets[None, :]

    def one_block(row):
        q_now = q_five[row, :, 0]
        own_k = k_blocks[row, :, 0]
        own_v = v_blocks[row, :, 0]
        doc_now = doc_query[row]
        own_scores = (
            jnp.einsum("mgd,nd->gmn", q_now, own_k, preferred_element_type=jnp.float32) * scale
        )
        sel_scores = (
            jnp.einsum("mgd,nd->gmn", q_now, chosen_k[row, 0], preferred_element_type=jnp.float32)
            * scale
        )
        own_mask = causal & (doc_now[:, None] == doc_now[None, :])
        sel_mask = (doc_now[:, None] == doc_chosen[row, 0][None, :]) & live[row, 0]
        top = jnp.maximum(
            jnp.max(jnp.where(own_mask, own_scores, -jnp.inf), axis=-1),
            jnp.max(jnp.where(sel_mask, sel_scores, -jnp.inf), axis=-1),
        )
        own_weight = jnp.where(own_mask, jnp.exp(own_scores - top[..., None]), 0.0)
        sel_weight = jnp.where(sel_mask, jnp.exp(sel_scores - top[..., None]), 0.0)
        total = jnp.sum(own_weight, axis=-1) + jnp.sum(sel_weight, axis=-1)
        acc = jnp.einsum(
            "gmn,nd->mgd",
            own_weight.astype(jnp.bfloat16),
            own_v,
            preferred_element_type=jnp.float32,
        )
        acc = acc + jnp.einsum(
            "gmn,nd->mgd",
            sel_weight.astype(jnp.bfloat16),
            chosen_v[row, 0],
            preferred_element_type=jnp.float32,
        )
        output = (acc / jnp.transpose(total)[:, :, None]).astype(jnp.bfloat16)
        results = [output.reshape(MB, group * HD)]
        return jnp.concatenate(results, axis=1)

    blocks = lax.map(one_block, jnp.arange(per_dev, dtype=jnp.int32))
    head_major = blocks.reshape(shard, kv_dev * group * HD)
    return lax.all_to_all(
        shortened(head_major), "uly", split_axis=0, concat_axis=1, tiled=True
    ).astype(head_major.dtype)


def solution(mesh):
    placed = (P(("blk", "uly"), None), P(("blk", "uly"), None), P(("blk", "uly"), None), P(), P())
    return jax.shard_map(
        on_device, mesh=mesh, in_specs=placed, out_specs=P(("blk", "uly"), None), check_vma=False
    )
```

profile of v0, /device:TPU:0, one launch (start us, length us, event | category | flops | bytes accessed | tf_op | source)
XLA Modules:
  0.0 339.3 jit_solution(10035589432104716026)
XLA Ops:
  6.5 1.3 copy.43
  7.8 15.3 %all_to_all.73 = bf16[256,8,128]{0,2,1:T(8,128)(2,1)S(1)} all-to-all(bf16[256,8,128]{0,2,1:T(8,128)(2,1)S(1)} %bitcast.166), channel_id=1, replica_groups=mesh['blk'=16,'uly'=8] {'uly'}, dimensions={1} | all-to-all | bytes 1048576 | tf_op jit(solution)/shard_map/all_to_all | solution.py:24
  24.4 11.7 %all_to_all.74 = bf16[256,8,128]{2,0,1:T(8,128)(2,1)} all-to-all(bf16[256,8,128]{2,0,1:T(8,128)(2,1)S(1)} %copy_bitcast_fusion.4), channel_id=1, replica_groups=mesh['blk'=16,'uly'=8] {'uly'}, dimensions={1} | all-to-all | bytes 1048576 | tf_op jit(solution)/shard_map/all_to_all | solution.py:23
  36.1 3.1 copy.80
  39.3 3.6 %all-to-all-start.2 = ((bf16[256,8,512]{2,0,1:T(8,128)(2,1)}), bf16[256,8,512]{2,0,1:T(8,128)(2,1)S(1)}, u32[]{:S(2)}, u32[]{:S(2)}) async-start(bf16[256,8,512]{2,0,1:T(8,128)(2,1)} %bitcast.154), calls=%async_computation.2 | async-start | bytes 4194304 | tf_op jit(solution)/shard_map/all_to_all | solution.py:22
  45.2 27.4 %all-to-all-done.2 = bf16[256,8,512]{2,0,1:T(8,128)(2,1)S(1)} async-done(((bf16[256,8,512]{2,0,1:T(8,128)(2,1)}), bf16[256,8,512]{2,0,1:T(8,128)(2,1)S(1)}, u32[]{:S(2)}, u32[]{:S(2)}) %all-to-all-start.2) | async-done | bytes 2097184 | tf_op jit(solution)/shard_map/all_to_all | solution.py:22
  72.6 2.1 reshape.225
  74.7 27.1 %all-gather.5.cloned.1.call-done = bf16[32768,128]{1,0:T(8,128)(2,1)} async-done(((bf16[2048,128]{1,0:T(8,128)(2,1)}), bf16[32768,128]{1,0:T(8,128)(2,1)}) %all-gather.5.cloned.1.call-update) | async-done | bytes 8388624 | tf_op jit(solution)/shard_map/all_gather | solution.py:45
  101.8 22.6 %gather_fusion.1 = bf16[2048,128]{1,0:T(8,128)(2,1)S(1)} fusion(bf16[32768,1,128]{2,0,1:T(8,128)(2,1)} %bitcast.157, s32[2048]{0:T(1024)S(1)} %bitcast.150), kind=kCustom, calls=%fused_computation.1 | custom fusion | bytes 1064960 | tf_op jit(solution)/shard_map/gather | solution.py:52
  124.7 50.9 %all-gather.3.cloned.1.call-done = bf16[32768,128]{1,0:T(8,128)(2,1)} async-done(((bf16[2048,128]{1,0:T(8,128)(2,1)}), bf16[32768,128]{1,0:T(8,128)(2,1)}) %all-gather.3.cloned.1.call-update) | async-done | bytes 8388624 | tf_op jit(solution)/shard_map/all_gather | solution.py:44
  175.6 22.6 %gather_fusion = bf16[2048,128]{1,0:T(8,128)(2,1)S(1)} fusion(bf16[32768,1,128]{2,0,1:T(8,128)(2,1)} %bitcast.158, s32[2048]{0:T(1024)S(1)} %bitcast.151), kind=kCustom, calls=%fused_computation | custom fusion | bytes 1064960 | tf_op jit(solution)/shard_map/gather | solution.py:51
  198.4 1.1 broadcast_select_fusion
  199.5 94.8 %while.11 = (s32[]{:T(128)}, bf16[2,1024,512]{2,1,0:T(8,128)(2,1)}, s32[2]{0:T(128)S(1)}, bf16[2,1024,1,128]{3,1,0,2:T(8,128)(2,1)S(1)}, s32[2,1024]{1,0:T(2,128...) while((s32[]{:T(128)}, bf16[2,1024,512]{2,1,0:T(8,128)(2,1)}, ...), condition=%wide.region_8.9_spmd.clone, body=%wide.region_3.8_spmd.clone.sunk | while | flops 4394049536 | bytes 123986648 | solution.py:98
  202.5 2.5 compare_and_fusion.3
  205.0 1.6 constant_dynamic-slice_fusion.11
  206.6 4.0 %fusion.59 = (f32[4,1024]{1,0:T(4,128)S(1)}, f32[1024,1024,4]{1,0,2:T(8,128)S(1)}) fusion(pred[1024,1024]{0,1:T(8,128)(4,1)S(1)} %get-tuple-element.245, bf16[1,1024,1,4,128]{4,3,1,0,2:T(4,128)(2,1)S(1)} %constant_dynamic-slice_fusion.11, bf16[2,1024,1,128]{3,1,2,0:T(8,128)(2,1)} %get-tuple-element.284, s32[]{:T(128)S(6)} %select_n.115), kind=kOutput, calls=%fused_computation.10.clone.1 | convolution fusion | flops 1086320640 | bytes 19152900 | tf_op jit(solution)/shard_map/while/body/eval_jaxpr/mgd,nd->gmn/dot_general | solution.py:67
  210.6 8.5 %fusion.58 = (f32[4,1024]{1,0:T(4,128)S(1)}, f32[1024,1024,4]{1,0,2:T(8,128)}) fusion(pred[1024,1024]{0,1:T(8,128)(4,1)S(1)} %get-tuple-element.243, bf16[1,1024,1,4,128]{4,3,1,0,2:T(4,128)(2,1)S(1)} %constant_dynamic-slice_fusion.11, bf16[2,1,1024,128]{2,3,1,0:T(8,128)(2,1)} %get-tuple-element.288, s32[]{:T(128)S(6)} %select_n.115), kind=kOutput, calls=%fused_computation.5.clone.1 | convolution fusion | flops 1086320640 | bytes 19152900 | tf_op jit(solution)/shard_map/while/body/eval_jaxpr/mgd,nd->gmn/dot_general | solution.py:70
  219.1 9.9 %fusion.61 = (f32[4,1024]{1,0:T(4,128)S(1)}, f32[4,1024]{1,0:T(4,128)S(1)}) fusion(f32[1024,1024,4]{1,0,2:T(8,128)} %get-tuple-element.244, f32[4,1024]{1,0:T(4,128)S(1)} %max.13, pred[1024,1024]{0,1:T(8,128)(4,1)S(1)} %get-tuple-element.243, f32[1024,1024,4]{1,0,2:T(8,128)S(1)} %get-tuple-element.248, pred[1024,1024]{0,1:T(8,128)(4,1)S(1)} %get-tuple-element.245), kind=kLoop, calls=%fused_computation.15.clone.1 | loop fusion | flops 33546240 | bytes 35700736 | tf_op jit(solution)/shard_map/while/body/eval_jaxpr/reduce_sum | solution.py:81
  229.1 11.0 %fusion.60 = f32[128,4,1024]{2,0,1:T(8,128)} fusion(f32[1024,1024,4]{1,0,2:T(8,128)} %get-tuple-element.244, f32[4,1024]{1,0:T(4,128)S(1)} %max.13, pred[1024,1024]{0,1:T(8,128)(4,1)S(1)} %get-tuple-element.243, bf16[2,1,1024,128]{2,3,1,0:T(8,128)(2,1)} %get-tuple-element.289, s32[]{:T(128)S(6)} %select_n.115), kind=kOutput, calls=%fused_computation.17.clone.1 | convolution fusion | flops 1090519040 | bytes 20201476 | tf_op jit(solution)/shard_map/while/body/eval_jaxpr/gmn,nd->mgd/dot_general | solution.py:88
  240.1 5.2 %fusion.62 = bf16[1024,4,128]{0,2,1:T(8,128)(2,1)S(1)} fusion(f32[128,4,1024]{2,0,1:T(8,128)} %fusion.60, f32[1024,1024,4]{1,0,2:T(8,128)S(1)} %get-tuple-element.248, f32[4,1024]{1,0:T(4,128)S(1)} %max.13, pred[1024,1024]{0,1:T(8,128)(4,1)S(1)} %get-tuple-element.245, f32[1024,4]{0,1:T(4,128)S(1)} %add_bitcast_fusion.2, ...), kind=kOutput, calls=%fused_computation.25.clone.1 | convolution fusion | flops 1092091904 | bytes 21266436 | tf_op jit(solution)/shard_map/while/body/eval_jaxpr/gmn,nd->mgd/dot_general | solution.py:82
  245.9 1.0 constant_dynamic-update-slice_fusion.2
  249.9 2.5 compare_and_fusion.3
  252.4 1.6 constant_dynamic-slice_fusion.11
  254.0 4.0 %fusion.59 = (f32[4,1024]{1,0:T(4,128)S(1)}, f32[1024,1024,4]{1,0,2:T(8,128)S(1)}) fusion(pred[1024,1024]{0,1:T(8,128)(4,1)S(1)} %get-tuple-element.245, bf16[1,1024,1,4,128]{4,3,1,0,2:T(4,128)(2,1)S(1)} %constant_dynamic-slice_fusion.11, bf16[2,1024,1,128]{3,1,2,0:T(8,128)(2,1)} %get-tuple-element.284, s32[]{:T(128)S(6)} %select_n.115), kind=kOutput, calls=%fused_computation.10.clone.1 | convolution fusion | flops 1086320640 | bytes 19152900 | tf_op jit(solution)/shard_map/while/body/eval_jaxpr/mgd,nd->gmn/dot_general | solution.py:67
  258.0 8.5 %fusion.58 = (f32[4,1024]{1,0:T(4,128)S(1)}, f32[1024,1024,4]{1,0,2:T(8,128)}) fusion(pred[1024,1024]{0,1:T(8,128)(4,1)S(1)} %get-tuple-element.243, bf16[1,1024,1,4,128]{4,3,1,0,2:T(4,128)(2,1)S(1)} %constant_dynamic-slice_fusion.11, bf16[2,1,1024,128]{2,3,1,0:T(8,128)(2,1)} %get-tuple-element.288, s32[]{:T(128)S(6)} %select_n.115), kind=kOutput, calls=%fused_computation.5.clone.1 | convolution fusion | flops 1086320640 | bytes 19152900 | tf_op jit(solution)/shard_map/while/body/eval_jaxpr/mgd,nd->gmn/dot_general | solution.py:70
  266.5 9.9 %fusion.61 = (f32[4,1024]{1,0:T(4,128)S(1)}, f32[4,1024]{1,0:T(4,128)S(1)}) fusion(f32[1024,1024,4]{1,0,2:T(8,128)} %get-tuple-element.244, f32[4,1024]{1,0:T(4,128)S(1)} %max.13, pred[1024,1024]{0,1:T(8,128)(4,1)S(1)} %get-tuple-element.243, f32[1024,1024,4]{1,0,2:T(8,128)S(1)} %get-tuple-element.248, pred[1024,1024]{0,1:T(8,128)(4,1)S(1)} %get-tuple-element.245), kind=kLoop, calls=%fused_computation.15.clone.1 | loop fusion | flops 33546240 | bytes 35700736 | tf_op jit(solution)/shard_map/while/body/eval_jaxpr/reduce_sum | solution.py:81
  276.5 11.0 %fusion.60 = f32[128,4,1024]{2,0,1:T(8,128)} fusion(f32[1024,1024,4]{1,0,2:T(8,128)} %get-tuple-element.244, f32[4,1024]{1,0:T(4,128)S(1)} %max.13, pred[1024,1024]{0,1:T(8,128)(4,1)S(1)} %get-tuple-element.243, bf16[2,1,1024,128]{2,3,1,0:T(8,128)(2,1)} %get-tuple-element.289, s32[]{:T(128)S(6)} %select_n.115), kind=kOutput, calls=%fused_computation.17.clone.1 | convolution fusion | flops 1090519040 | bytes 20201476 | tf_op jit(solution)/shard_map/while/body/eval_jaxpr/gmn,nd->mgd/dot_general | solution.py:88
  287.4 5.2 %fusion.62 = bf16[1024,4,128]{0,2,1:T(8,128)(2,1)S(1)} fusion(f32[128,4,1024]{2,0,1:T(8,128)} %fusion.60, f32[1024,1024,4]{1,0,2:T(8,128)S(1)} %get-tuple-element.248, f32[4,1024]{1,0:T(4,128)S(1)} %max.13, pred[1024,1024]{0,1:T(8,128)(4,1)S(1)} %get-tuple-element.245, f32[1024,4]{0,1:T(4,128)S(1)} %add_bitcast_fusion.2, ...), kind=kOutput, calls=%fused_computation.25.clone.1 | convolution fusion | flops 1092091904 | bytes 21266436 | tf_op jit(solution)/shard_map/while/body/eval_jaxpr/gmn,nd->mgd/dot_general | solution.py:82
  293.2 1.0 constant_dynamic-update-slice_fusion.2
  294.3 31.7 %all_to_all.75 = bf16[8,256,512]{2,1,0:T(8,128)(2,1)S(1)} all-to-all(bf16[8,256,512]{2,1,0:T(8,128)(2,1)} %bitcast.160), channel_id=1, replica_groups=mesh['blk'=16,'uly'=8] {'uly'}, dimensions={0} | all-to-all | bytes 4194304 | tf_op jit(solution)/shard_map/all_to_all | solution.py:100
  326.0 2.4 copy.56
  328.4 4.1 %copy.57 = bf16[256,4096]{1,0:T(8,128)(2,1)} copy(bf16[256,4096]{0,1:T(8,128)(2,1)} %bitcast.156) | data formatting | bytes 4194304 | tf_op jit(solution)/shard_map/all_to_all | solution.py:100
  (45 shorter events, 7.4 us)
Async XLA Ops:
  6.5 17.7 %copy-start = (bf16[256,1024]{1,0:T(8,128)(2,1)S(1)}, bf16[256,1024]{1,0:T(8,128)(2,1)}, u32[]{:S(2)}) copy-start(bf16[256,1024]{1,0:T(8,128)(2,1)} %param.8) | copy-start | bytes 1572868
  6.5 95.3 %all-gather.5.cloned.1.call-start = ((), (), s32[]{:S(2)}) async-start(), calls=%async_computation.5 | async-start | bytes 8912896 | tf_op jit(solution)/shard_map/all_gather | solution.py:45
  24.2 175.3 %copy-start.2 = (bf16[8,256,128]{2,1,0:T(8,128)(2,1)S(1)}, bf16[8,256,128]{2,1,0:T(8,128)(2,1)}, u32[]{:S(2)}) copy-start(bf16[8,256,128]{2,1,0:T(8,128)(2,1)} %copy.44) | copy-start | bytes 1572868
  24.2 151.4 %all-gather.3.cloned.1.call-start = ((), (), s32[]{:S(2)}) async-start(), calls=%async_computation.4 | async-start | bytes 8912896 | tf_op jit(solution)/shard_map/all_gather | solution.py:44
  39.3 33.4 %all-to-all-start.2 = ((bf16[256,8,512]{2,0,1:T(8,128)(2,1)}), bf16[256,8,512]{2,0,1:T(8,128)(2,1)S(1)}, u32[]{:S(2)}, u32[]{:S(2)}) async-start(bf16[256,8,512]{2,0,1:T(8,128)(2,1)} %bitcast.154), calls=%async_computation.2 | async-start | bytes 4194304 | tf_op jit(solution)/shard_map/all_to_all | solution.py:22
  294.3 38.1 %copy-start.1 = (bf16[256,1024]{1,0:T(8,128)(2,1)S(1)}, bf16[256,1024]{1,0:T(8,128)(2,1)}, u32[]{:S(2)}) copy-start(bf16[256,1024]{1,0:T(8,128)(2,1)} %param.8) | copy-start | bytes 1572868
Sparse Core Ops, SparseCore 0:
  24.3 77.4 all-gather.4
  104.3 71.2 all-gather.2
where the time goes:
time: 341 us; the launch traced here: 339 us
  waiting for transfers between devices  105 us (31%)
  local copies, waits for them, and re-layouts  69.3 us (20%)
  blocking collectives  58.8 us (17%)
  matrix products  57.4 us (17%)
  other arithmetic  27.3 us (8%)
  between operations  13.5 us (4%)
  loops' own time  3.8 us (1%)
  starting transfers between devices  3.65 us (1%)
    all_gather x1, waiting for transfers between devices, on_device(): k_piece = lax.all_gather(k_heads, 'blk', axis=0, tiled=True)  50.9 us
    all_to_all x1, blocking collectives, on_device(): lax.all_to_all(shortened(head_major), 'uly', split_axis=0, concat_axis=1,...  31.7 us
    all_to_all x1, waiting for transfers between devices, on_device(): lax.all_to_all(queries, 'uly', split_axis=1, concat_axis=0, tiled=True)  27.4 us
    all_gather x1, waiting for transfers between devices, on_device(): v_piece = lax.all_gather(v_heads, 'blk', axis=0, tiled=True)  27.1 us
    gather x2, local copies, waits for them, and re-layouts, on_device(): v_got = v_piece.reshape(count, kv_dev, HD)[index, head_rows]  22.8 us
    gather x2, local copies, waits for them, and re-layouts, on_device(): k_got = k_piece.reshape(count, kv_dev, HD)[index, head_rows]  22.8 us
    dot_general x2, matrix products, one_block(): jnp.einsum('gmn,nd->mgd', sel_weight.astype(jnp.bfloat16), chosen_v[row,...  21.9 us
    reduce_sum x2, other arithmetic, one_block(): total = jnp.sum(own_weight, axis=-1) + jnp.sum(sel_weight, axis=-1)  19.9 us
  transfers between devices with their start and end apart: 3, of which 3 were waited for; matrix products, arithmetic and copies ran while one was open for 9% of the time, Pallas kernels for 0%

commit v1 on v0

--- a/solution.py
+++ b/solution.py
@@ -7,6 +7,13 @@
 KVH = 8
 HD = 128
 MB = 1024
+
+
+def exchange_blocks(x, axis, split, join):
+    devices = lax.axis_size(axis)
+    blocks = jnp.stack(jnp.split(x, devices, axis=split), axis=0)
+    blocks = lax.all_to_all(blocks, axis, split_axis=0, concat_axis=0)
+    return jnp.concatenate(blocks, axis=join)
 
 
 def shortened(shard):
@@ -19,7 +26,7 @@
 
 def on_device(queries, keys, values, doc_lengths, selected):
     q_heads, k_heads, v_heads = (
-        lax.all_to_all(queries, "uly", split_axis=1, concat_axis=0, tiled=True),
+        exchange_blocks(queries, "uly", 1, 0),
         lax.all_to_all(keys, "uly", split_axis=1, concat_axis=0, tiled=True),
         lax.all_to_all(values, "uly", split_axis=1, concat_axis=0, tiled=True),
     )

time: 341 us -> 344 us (level)
  local copies, waits for them, and re-layouts: 69.3 us -> 72.9 us
    unnamed x9 -> x20, local copies, waits for them, and re-layouts: 1.41 us -> 7.41 us
where the time goes in v1:
time: 344 us; the launch traced here: 343 us
  waiting for transfers between devices  106 us (31%)
  local copies, waits for them, and re-layouts  72.9 us (21%)
  blocking collectives  58.8 us (17%)
  matrix products  57.4 us (17%)
  other arithmetic  26.7 us (8%)
  between operations  13.6 us (4%)
  loops' own time  3.8 us (1%)
  starting transfers between devices  3.65 us (1%)
    all_gather x1, waiting for transfers between devices, on_device(): k_piece = lax.all_gather(k_heads, 'blk', axis=0, tiled=True)  51 us
    all_to_all x1, blocking collectives, on_device(): lax.all_to_all(shortened(head_major), 'uly', split_axis=0, concat_axis=1,...  31.5 us
    all_to_all x1, waiting for transfers between devices, exchange_blocks(): blocks = lax.all_to_all(blocks, axis, split_axis=0, concat_axis=0)  30.7 us
    all_gather x1, waiting for transfers between devices, on_device(): v_piece = lax.all_gather(v_heads, 'blk', axis=0, tiled=True)  24.3 us
    gather x2, local copies, waits for them, and re-layouts, on_device(): v_got = v_piece.reshape(count, kv_dev, HD)[index, head_rows]  22.8 us
    gather x2, local copies, waits for them, and re-layouts, on_device(): k_got = k_piece.reshape(count, kv_dev, HD)[index, head_rows]  22.8 us
    dot_general x2, matrix products, one_block(): jnp.einsum('gmn,nd->mgd', sel_weight.astype(jnp.bfloat16), chosen_v[row,...  21.9 us
    reduce_sum x2, other arithmetic, one_block(): total = jnp.sum(own_weight, axis=-1) + jnp.sum(sel_weight, axis=-1)  19.9 us
  transfers between devices with their start and end apart: 3, of which 3 were waited for; matrix products, arithmetic and copies ran while one was open for 9% of the time, Pallas kernels for 0%

profile of v1, /device:TPU:0, one launch (start us, length us, event | category | flops | bytes accessed | tf_op | source)
XLA Modules:
  0.0 342.8 jit_solution(9090520632633852566)
XLA Ops:
  6.5 2.2 copy.41
  8.7 15.5 %all_to_all.62 = bf16[256,8,128]{0,2,1:T(8,128)(2,1)S(1)} all-to-all(bf16[256,8,128]{0,2,1:T(8,128)(2,1)} %bitcast.172), channel_id=1, replica_groups=mesh['blk'=16,'uly'=8] {'uly'}, dimensions={1} | all-to-all | bytes 1048576 | tf_op jit(solution)/shard_map/all_to_all | solution.py:31
  24.3 1.0 copy.42
  25.5 11.7 %all_to_all.63 = bf16[256,8,128]{2,0,1:T(8,128)(2,1)} all-to-all(bf16[256,8,128]{2,0,1:T(8,128)(2,1)S(1)} %copy_bitcast_fusion.3), channel_id=1, replica_groups=mesh['blk'=16,'uly'=8] {'uly'}, dimensions={1} | all-to-all | bytes 1048576 | tf_op jit(solution)/shard_map/all_to_all | solution.py:30
  43.1 3.6 %all-to-all-start.2 = ((bf16[8,256,512]{2,1,0:T(8,128)(2,1)}), bf16[8,256,512]{2,1,0:T(8,128)(2,1)S(1)}, u32[]{:S(2)}, u32[]{:S(2)}) async-start(bf16[8,256,512]{2,1,0:T(8,128)(2,1)} %bitcast_dynamic-update-slice_fusion), calls=%async_computation.2 | async-start | bytes 4194304 | tf_op jit(solution)/shard_map/all_to_all | solution.py:15
  48.4 30.7 %all-to-all-done.2 = bf16[8,256,512]{2,1,0:T(8,128)(2,1)S(1)} async-done(((bf16[8,256,512]{2,1,0:T(8,128)(2,1)}), bf16[8,256,512]{2,1,0:T(8,128)(2,1)S(1)}, u32[]{:S(2)}, u32[]{:S(2)}) %all-to-all-start.2) | async-done | bytes 2097184 | tf_op jit(solution)/shard_map/all_to_all | solution.py:15
  79.1 2.1 reshape_reshape.3
  81.1 24.3 %all-gather.5.cloned.1.call-done = bf16[32768,128]{1,0:T(8,128)(2,1)} async-done(((bf16[2048,128]{1,0:T(8,128)(2,1)}), bf16[32768,128]{1,0:T(8,128)(2,1)}) %all-gather.5.cloned.1.call-update) | async-done | bytes 8388624 | tf_op jit(solution)/shard_map/all_gather | solution.py:52
  105.4 22.6 %gather_fusion.1 = bf16[2048,128]{1,0:T(8,128)(2,1)S(1)} fusion(bf16[32768,1,128]{2,0,1:T(8,128)(2,1)} %bitcast.166, s32[2048]{0:T(1024)S(1)} %bitcast.161), kind=kCustom, calls=%fused_computation.1 | custom fusion | bytes 1064960 | tf_op jit(solution)/shard_map/gather | solution.py:59
  128.3 51.0 %all-gather.3.cloned.1.call-done = bf16[32768,128]{1,0:T(8,128)(2,1)} async-done(((bf16[2048,128]{1,0:T(8,128)(2,1)}), bf16[32768,128]{1,0:T(8,128)(2,1)}) %all-gather.3.cloned.1.call-update) | async-done | bytes 8388624 | tf_op jit(solution)/shard_map/all_gather | solution.py:51
  179.3 22.6 %gather_fusion = bf16[2048,128]{1,0:T(8,128)(2,1)S(1)} fusion(bf16[32768,1,128]{2,0,1:T(8,128)(2,1)} %bitcast.167, s32[2048]{0:T(1024)S(1)} %bitcast.162), kind=kCustom, calls=%fused_computation | custom fusion | bytes 1064960 | tf_op jit(solution)/shard_map/gather | solution.py:58
  202.1 1.1 broadcast_select_fusion
  203.2 94.8 %while.11 = (s32[]{:T(128)}, bf16[2,1024,512]{2,1,0:T(8,128)(2,1)}, s32[2]{0:T(128)S(1)}, bf16[2,1024,1,128]{3,1,0,2:T(8,128)(2,1)S(1)}, s32[2,1024]{1,0:T(2,128...) while((s32[]{:T(128)}, bf16[2,1024,512]{2,1,0:T(8,128)(2,1)}, ...), condition=%wide.region_8.9_spmd.clone, body=%wide.region_3.8_spmd.clone.sunk | while | flops 4394049536 | bytes 123986648 | solution.py:105
  206.2 2.5 compare_and_fusion.3
  208.7 1.6 constant_dynamic-slice_fusion.11
  210.3 4.0 %fusion.59 = (f32[4,1024]{1,0:T(4,128)S(1)}, f32[1024,1024,4]{1,0,2:T(8,128)S(1)}) fusion(pred[1024,1024]{0,1:T(8,128)(4,1)S(1)} %get-tuple-element.245, bf16[1,1024,1,4,128]{4,3,1,0,2:T(4,128)(2,1)S(1)} %constant_dynamic-slice_fusion.11, bf16[2,1024,1,128]{3,1,2,0:T(8,128)(2,1)} %get-tuple-element.284, s32[]{:T(128)S(6)} %select_n.115), kind=kOutput, calls=%fused_computation.10.clone.1 | convolution fusion | flops 1086320640 | bytes 19152900 | tf_op jit(solution)/shard_map/while/body/eval_jaxpr/mgd,nd->gmn/dot_general | solution.py:74
  214.3 8.5 %fusion.58 = (f32[4,1024]{1,0:T(4,128)S(1)}, f32[1024,1024,4]{1,0,2:T(8,128)}) fusion(pred[1024,1024]{0,1:T(8,128)(4,1)S(1)} %get-tuple-element.243, bf16[1,1024,1,4,128]{4,3,1,0,2:T(4,128)(2,1)S(1)} %constant_dynamic-slice_fusion.11, bf16[2,1,1024,128]{2,3,1,0:T(8,128)(2,1)} %get-tuple-element.288, s32[]{:T(128)S(6)} %select_n.115), kind=kOutput, calls=%fused_computation.5.clone.1 | convolution fusion | flops 1086320640 | bytes 19152900 | tf_op jit(solution)/shard_map/while/body/eval_jaxpr/mgd,nd->gmn/dot_general | solution.py:77
  222.8 9.9 %fusion.61 = (f32[4,1024]{1,0:T(4,128)S(1)}, f32[4,1024]{1,0:T(4,128)S(1)}) fusion(f32[1024,1024,4]{1,0,2:T(8,128)} %get-tuple-element.244, f32[4,1024]{1,0:T(4,128)S(1)} %max.13, pred[1024,1024]{0,1:T(8,128)(4,1)S(1)} %get-tuple-element.243, f32[1024,1024,4]{1,0,2:T(8,128)S(1)} %get-tuple-element.248, pred[1024,1024]{0,1:T(8,128)(4,1)S(1)} %get-tuple-element.245), kind=kLoop, calls=%fused_computation.15.clone.1 | loop fusion | flops 33546240 | bytes 35700736 | tf_op jit(solution)/shard_map/while/body/eval_jaxpr/reduce_sum | solution.py:88
  232.8 11.0 %fusion.60 = f32[128,4,1024]{2,0,1:T(8,128)} fusion(f32[1024,1024,4]{1,0,2:T(8,128)} %get-tuple-element.244, f32[4,1024]{1,0:T(4,128)S(1)} %max.13, pred[1024,1024]{0,1:T(8,128)(4,1)S(1)} %get-tuple-element.243, bf16[2,1,1024,128]{2,3,1,0:T(8,128)(2,1)} %get-tuple-element.289, s32[]{:T(128)S(6)} %select_n.115), kind=kOutput, calls=%fused_computation.17.clone.1 | convolution fusion | flops 1090519040 | bytes 20201476 | tf_op jit(solution)/shard_map/while/body/eval_jaxpr/gmn,nd->mgd/dot_general | solution.py:95
  243.7 5.2 %fusion.62 = bf16[1024,4,128]{0,2,1:T(8,128)(2,1)S(1)} fusion(f32[128,4,1024]{2,0,1:T(8,128)} %fusion.60, f32[1024,1024,4]{1,0,2:T(8,128)S(1)} %get-tuple-element.248, f32[4,1024]{1,0:T(4,128)S(1)} %max.13, pred[1024,1024]{0,1:T(8,128)(4,1)S(1)} %get-tuple-element.245, f32[1024,4]{0,1:T(4,128)S(1)} %add_bitcast_fusion.2, ...), kind=kOutput, calls=%fused_computation.25.clone.1 | convolution fusion | flops 1092091904 | bytes 21266436 | tf_op jit(solution)/shard_map/while/body/eval_jaxpr/gmn,nd->mgd/dot_general | solution.py:89
  249.6 1.0 constant_dynamic-update-slice_fusion.2
  253.6 2.5 compare_and_fusion.3
  256.1 1.6 constant_dynamic-slice_fusion.11
  257.7 4.0 %fusion.59 = (f32[4,1024]{1,0:T(4,128)S(1)}, f32[1024,1024,4]{1,0,2:T(8,128)S(1)}) fusion(pred[1024,1024]{0,1:T(8,128)(4,1)S(1)} %get-tuple-element.245, bf16[1,1024,1,4,128]{4,3,1,0,2:T(4,128)(2,1)S(1)} %constant_dynamic-slice_fusion.11, bf16[2,1024,1,128]{3,1,2,0:T(8,128)(2,1)} %get-tuple-element.284, s32[]{:T(128)S(6)} %select_n.115), kind=kOutput, calls=%fused_computation.10.clone.1 | convolution fusion | flops 1086320640 | bytes 19152900 | tf_op jit(solution)/shard_map/while/body/eval_jaxpr/mgd,nd->gmn/dot_general | solution.py:74
  261.7 8.5 %fusion.58 = (f32[4,1024]{1,0:T(4,128)S(1)}, f32[1024,1024,4]{1,0,2:T(8,128)}) fusion(pred[1024,1024]{0,1:T(8,128)(4,1)S(1)} %get-tuple-element.243, bf16[1,1024,1,4,128]{4,3,1,0,2:T(4,128)(2,1)S(1)} %constant_dynamic-slice_fusion.11, bf16[2,1,1024,128]{2,3,1,0:T(8,128)(2,1)} %get-tuple-element.288, s32[]{:T(128)S(6)} %select_n.115), kind=kOutput, calls=%fused_computation.5.clone.1 | convolution fusion | flops 1086320640 | bytes 19152900 | tf_op jit(solution)/shard_map/while/body/eval_jaxpr/mgd,nd->gmn/dot_general | solution.py:77
  270.2 9.9 %fusion.61 = (f32[4,1024]{1,0:T(4,128)S(1)}, f32[4,1024]{1,0:T(4,128)S(1)}) fusion(f32[1024,1024,4]{1,0,2:T(8,128)} %get-tuple-element.244, f32[4,1024]{1,0:T(4,128)S(1)} %max.13, pred[1024,1024]{0,1:T(8,128)(4,1)S(1)} %get-tuple-element.243, f32[1024,1024,4]{1,0,2:T(8,128)S(1)} %get-tuple-element.248, pred[1024,1024]{0,1:T(8,128)(4,1)S(1)} %get-tuple-element.245), kind=kLoop, calls=%fused_computation.15.clone.1 | loop fusion | flops 33546240 | bytes 35700736 | tf_op jit(solution)/shard_map/while/body/eval_jaxpr/reduce_sum | solution.py:88
  280.2 11.0 %fusion.60 = f32[128,4,1024]{2,0,1:T(8,128)} fusion(f32[1024,1024,4]{1,0,2:T(8,128)} %get-tuple-element.244, f32[4,1024]{1,0:T(4,128)S(1)} %max.13, pred[1024,1024]{0,1:T(8,128)(4,1)S(1)} %get-tuple-element.243, bf16[2,1,1024,128]{2,3,1,0:T(8,128)(2,1)} %get-tuple-element.289, s32[]{:T(128)S(6)} %select_n.115), kind=kOutput, calls=%fused_computation.17.clone.1 | convolution fusion | flops 1090519040 | bytes 20201476 | tf_op jit(solution)/shard_map/while/body/eval_jaxpr/gmn,nd->mgd/dot_general | solution.py:95
  291.1 5.2 %fusion.62 = bf16[1024,4,128]{0,2,1:T(8,128)(2,1)S(1)} fusion(f32[128,4,1024]{2,0,1:T(8,128)} %fusion.60, f32[1024,1024,4]{1,0,2:T(8,128)S(1)} %get-tuple-element.248, f32[4,1024]{1,0:T(4,128)S(1)} %max.13, pred[1024,1024]{0,1:T(8,128)(4,1)S(1)} %get-tuple-element.245, f32[1024,4]{0,1:T(4,128)S(1)} %add_bitcast_fusion.2, ...), kind=kOutput, calls=%fused_computation.25.clone.1 | convolution fusion | flops 1092091904 | bytes 21266436 | tf_op jit(solution)/shard_map/while/body/eval_jaxpr/gmn,nd->mgd/dot_general | solution.py:89
  296.9 1.0 constant_dynamic-update-slice_fusion.2
  298.0 31.5 %all_to_all.64 = bf16[8,256,512]{2,1,0:T(8,128)(2,1)S(1)} all-to-all(bf16[8,256,512]{2,1,0:T(8,128)(2,1)} %bitcast.168), channel_id=1, replica_groups=mesh['blk'=16,'uly'=8] {'uly'}, dimensions={0} | all-to-all | bytes 4194304 | tf_op jit(solution)/shard_map/all_to_all | solution.py:107
  329.5 2.4 copy.53
  331.9 4.1 %copy.54 = bf16[256,4096]{1,0:T(8,128)(2,1)} copy(bf16[256,4096]{0,1:T(8,128)(2,1)} %bitcast.165) | data formatting | bytes 4194304 | tf_op jit(solution)/shard_map/all_to_all | solution.py:107
  (56 shorter events, 11.6 us)
Async XLA Ops:
  6.5 18.8 %copy-start = (bf16[256,1024]{1,0:T(8,128)(2,1)S(1)}, bf16[256,1024]{1,0:T(8,128)(2,1)}, u32[]{:S(2)}) copy-start(bf16[256,1024]{1,0:T(8,128)(2,1)} %param.8) | copy-start | bytes 1572868
  6.5 30.7 %copy-start.2 = (bf16[256,4096]{1,0:T(8,128)(2,1)S(1)}, bf16[256,4096]{1,0:T(8,128)(2,1)}, u32[]{:S(2)}) copy-start(bf16[256,4096]{1,0:T(8,128)(2,1)} %param.7) | copy-start | bytes 6291460
  6.5 98.9 %all-gather.5.cloned.1.call-start = ((), (), s32[]{:S(2)}) async-start(), calls=%async_computation.5 | async-start | bytes 8912896 | tf_op jit(solution)/shard_map/all_gather | solution.py:52
  25.3 154.0 %all-gather.3.cloned.1.call-start = ((), (), s32[]{:S(2)}) async-start(), calls=%async_computation.4 | async-start | bytes 8912896 | tf_op jit(solution)/shard_map/all_gather | solution.py:51
  37.2 10.6 %copy-start.4 = (s32[4]{0:T(128)S(1)}, s32[4]{0:T(128)}, u32[]{:S(2)}) copy-start(s32[4]{0:T(128)} %param.10) | copy-start | bytes 52
  43.1 36.0 %all-to-all-start.2 = ((bf16[8,256,512]{2,1,0:T(8,128)(2,1)}), bf16[8,256,512]{2,1,0:T(8,128)(2,1)S(1)}, u32[]{:S(2)}, u32[]{:S(2)}) async-start(bf16[8,256,512]{2,1,0:T(8,128)(2,1)} %bitcast_dynamic-update-slice_fusion), calls=%async_computation.2 | async-start | bytes 4194304 | tf_op jit(solution)/shard_map/all_to_all | solution.py:15
  179.3 23.9 %copy-start.3 = (bf16[8,256,128]{2,1,0:T(8,128)(2,1)S(1)}, bf16[8,256,128]{2,1,0:T(8,128)(2,1)}, u32[]{:S(2)}) copy-start(bf16[8,256,128]{2,1,0:T(8,128)(2,1)} %copy.42) | copy-start | bytes 1572868
  329.5 6.4 %copy-start.1 = (bf16[256,1024]{1,0:T(8,128)(2,1)S(1)}, bf16[256,1024]{1,0:T(8,128)(2,1)}, u32[]{:S(2)}) copy-start(bf16[256,1024]{1,0:T(8,128)(2,1)} %param.8) | copy-start | bytes 1572868
Sparse Core Ops, SparseCore 0:
  25.4 79.9 all-gather.4
  107.9 71.3 all-gather.2
